TPU v7x, 32 devices: a whole 2x2x4 slice. The times are simulated.
32 devices in a mesh: seg: 16 (over z, x, core), blk: 2 (over y).
Axes of the slice: x: 2, y: 2, z: 4, core: 2. Of those that a mesh axis runs over, the one named last changes fastest.
Arguments:
- queries: bfloat16 [4096, 2048], P(('seg', 'blk')), may hold values from -6 to 6
- keys: bfloat16 [4096, 2048], P(('seg', 'blk')), may hold values from -6 to 6
- values: bfloat16 [4096, 2048], P(('seg', 'blk')), may hold values from -6 to 6
- mid_offset: int32 [16], replicated, may hold values from 0 to 15, as said below
- far_offset: int32 [16], replicated, may hold values from 0 to 127, as said below
Outputs:
- attended: bfloat16 [4096, 2048], P(('seg', 'blk'))
Inputs may be any that keep to these rules, and one draw needn't show every extreme that they name: `mid_offset`: one head has offset 0 and another 16 - 1. `far_offset`: one head has offset 0 and another 128 - 1.
All inputs are finite; a program needn't handle non-finite values.
Results may differ from a plain program's by a relative error of at most 0.0065.
Values may be sent and summed in bfloat16 or wider, within the bound.
A program may use at most 64 MiB of HBM per device.

v0:
```python
import math

import jax
import jax.numpy as jnp
from jax import lax
from jax.sharding import PartitionSpec as P

HEADS = 16
DH = 128
SPAN = 4
MID_RATE = 16


very_low = -1e30


def from_partner(shard, axis, bit):
    return lax.ppermute(shard, axis, [(i, i ^ 1 << bit) for i in range(lax.axis_size(axis))])


def attend_direct(query_rows, key_rows, value_rows):
    score_scale = 1.0 / math.sqrt(query_rows.shape[-1])
    scores = (
        jnp.einsum("qhd,khd->hqk", query_rows, key_rows, preferred_element_type=jnp.float32)
        * score_scale
    )
    row_top = jnp.max(scores, axis=-1)
    weights = jnp.exp(scores - row_top[..., None])
    totals = jnp.sum(weights, axis=-1)
    mixed = jnp.einsum(
        "hqk,khd->qhd", weights.astype(jnp.bfloat16), value_rows, preferred_element_type=jnp.float32
    )
    return (mixed / jnp.transpose(totals)[..., None], jnp.transpose(row_top + jnp.log(totals)))


def online_start(heads, rows, dims):
    return (
        jnp.full((heads, rows), very_low, jnp.float32),
        jnp.zeros((heads, rows), jnp.float32),
        jnp.zeros((heads, rows, dims), jnp.float32),
    )


def online_step(state_now, query_rows, key_rows, value_rows):
    row_top, totals, mixed = state_now
    score_scale = 1.0 / math.sqrt(query_rows.shape[-1])
    scores = (
        jnp.einsum("qhd,khd->hqk", query_rows, key_rows, preferred_element_type=jnp.float32)
        * score_scale
    )
    new_top = jnp.maximum(row_top, jnp.max(scores, axis=-1))
    weights = jnp.exp(scores - new_top[..., None])
    totals = jnp.sum(weights, axis=-1)
    mixed = jnp.einsum(
        "hqk,khd->hqd", weights.astype(jnp.bfloat16), value_rows, preferred_element_type=jnp.float32
    )
    return (new_top, totals, mixed)


def online_finish(state_now):
    row_top, totals, mixed = state_now
    level_out = jnp.transpose(mixed / totals[..., None], (1, 0, 2))
    return (level_out, jnp.transpose(row_top + jnp.log(totals)))


def combine_levels(
    dense_out, dense_lse, mid_out, mid_lse, far_out, far_lse, mid_offset, far_offset
):
    rows = dense_out.shape[0]
    heads = dense_out.shape[1]
    dims = dense_out.shape[2]
    rate = rows // mid_out.shape[0]
    mid_hit = jnp.arange(rate, dtype=jnp.int32)[:, None] == mid_offset[None, :]
    mid_full = jnp.where(mid_hit[None, :, :, None], mid_out[:, None], 0.0).reshape(
        rows, heads, dims
    )
    mid_lse_full = jnp.where(mid_hit[None], mid_lse[:, None, :], very_low).reshape(rows, heads)
    far_hit = jnp.arange(rows, dtype=jnp.int32)[:, None] == far_offset[None, :]
    far_full = jnp.where(far_hit[..., None], far_out[None], 0.0)
    far_lse_full = jnp.where(far_hit, far_lse[None], very_low)
    level_top = jnp.maximum(dense_lse, jnp.maximum(mid_lse_full, far_lse_full))
    dense_weight = jnp.exp(dense_lse - level_top)
    mid_weight = jnp.exp(mid_lse_full - level_top)
    far_weight = jnp.exp(far_lse_full - level_top)
    mixed = (
        dense_weight[..., None] * dense_out
        + mid_weight[..., None] * mid_full
        + far_weight[..., None] * far_full
    )
    mixed = mixed / (dense_weight + mid_weight + far_weight)[..., None]
    return mixed.astype(jnp.bfloat16).reshape(rows, heads * dims)


def on_device(queries, keys, values, mid_offset, far_offset):
    rows = queries.shape[0]
    query_rows = queries.reshape(rows, HEADS, DH)
    key_rows = keys.reshape(rows, HEADS, DH)
    value_rows = values.reshape(rows, HEADS, DH)
    piece_rows = (
        lax.all_gather(keys, "blk", axis=0, tiled=True),
        lax.all_gather(values, "blk", axis=0, tiled=True),
    )
    key_piece = piece_rows[0].reshape(-1, HEADS, DH)
    value_piece = piece_rows[1].reshape(-1, HEADS, DH)
    dense_state = online_step(online_start(HEADS, rows, DH), query_rows, key_piece, value_piece)
    dense_out, dense_lse = online_finish(dense_state)
    mid_select = (jnp.arange(MID_RATE, dtype=jnp.int32)[:, None] == mid_offset[None, :]).astype(
        jnp.bfloat16
    )

    def pick_mid(field):
        shaped = field.reshape(rows // MID_RATE, MID_RATE, HEADS, DH)
        return jnp.einsum(
            "jrhd,rh->jhd", shaped, mid_select, preferred_element_type=jnp.float32
        ).astype(jnp.bfloat16)

    mid_pairs = jnp.stack([pick_mid(key_rows), pick_mid(value_rows)])
    bit_count = SPAN.bit_length() - 1
    mid_pairs = lax.all_gather(mid_pairs, "blk", axis=1, tiled=True)
    for bit_index in range(bit_count):
        partner_rows = from_partner(mid_pairs, "seg", bit_index)
        mid_pairs = jnp.concatenate([mid_pairs, partner_rows], axis=1)
    mid_out, mid_lse = attend_direct(pick_mid(query_rows), mid_pairs[0], mid_pairs[1])
    far_select = (jnp.arange(rows, dtype=jnp.int32)[:, None] == far_offset[None, :]).astype(
        jnp.bfloat16
    )

    def pick_far(field):
        return jnp.einsum(
            "thd,th->hd", field, far_select, preferred_element_type=jnp.float32
        ).astype(jnp.bfloat16)[None]

    far_pairs = jnp.stack([pick_far(key_rows), pick_far(value_rows)])
    far_query = pick_far(query_rows)
    piece_rows = lax.all_gather(far_pairs, ("seg", "blk"), axis=1, tiled=True)
    far_state = online_step(online_start(HEADS, 1, DH), far_query, piece_rows[0], piece_rows[1])
    far_out, far_lse = online_finish(far_state)
    return combine_levels(
        dense_out, dense_lse, mid_out, mid_lse, far_out[0], far_lse[0], mid_offset, far_offset
    )


def solution(mesh):
    return jax.shard_map(
        on_device,
        mesh=mesh,
        in_specs=(
            P(("seg", "blk"), None),
            P(("seg", "blk"), None),
            P(("seg", "blk"), None),
            P(),
            P(),
        ),
        out_specs=P(("seg", "blk"), None),
        check_vma=False,
    )
```

profile of v0, /device:TPU:0, one launch (start us, length us, event | category | flops | bytes accessed | tf_op | source)
XLA Modules:
  0.0 114.1 jit_solution(16395666675392113394)
XLA Ops:
  6.5 0.0 copy-start.1
  6.5 0.0 copy-start.4
  6.5 0.0 all-gather.3.cloned.1.call-start
  6.5 2.1 %copy.17 = bf16[128,2048]{0,1:T(8,128)(2,1)} copy(bf16[128,2048]{1,0:T(8,128)(2,1)} %param.6) | data formatting | bytes 1048576 | tf_op args[1]
  8.6 0.0 all-gather.3.cloned.1.call-update
  8.7 0.0 all-gather.5.cloned.1.call-start
  8.7 0.0 copy-start.3
  8.7 0.0 copy-start.2
  8.7 1.2 %copy.49 = bf16[16,8,16,128]{3,2,1,0:T(8,128)(2,1)S(1)} copy(bf16[16,8,16,128]{3,1,2,0:T(8,128)(2,1)} %bitcast.150) | data formatting | bytes 1048576
  10.0 0.0 copy-done.1
  10.0 0.0 copy-start
  10.0 0.1 copy.48
  10.1 0.0 copy-done.4
  10.1 0.1 iota_compare_fusion.1
  10.2 0.2 fusion.22
  10.4 0.2 fusion.24
  10.7 5.9 %all_gather.13 = bf16[2,16,16,128]{3,1,2,0:T(8,128)(2,1)S(1)} all-gather(bf16[2,8,16,128]{3,1,2,0:T(8,128)(2,1)S(1)} %pad_maximum_fusion.1), channel_id=1, replica_groups=mesh['seg'=16,'blk'=2] {'blk'}, dimensions={1}, use_global_device_ids=true | all-gather | bytes 196608 | tf_op jit(solution)/shard_map/all_gather | solution.py:119
  16.6 0.0 collective-permute-start
  16.6 0.0 all-gather.5.cloned.1.call-update
  16.6 0.0 copy-done.3
  16.6 0.1 iota_compare_fusion
  16.7 0.0 copy-done.2
  16.7 0.2 fusion.12
  16.9 0.3 fusion.15
  17.2 0.0 copy-done
  17.2 0.3 fusion.18
  17.4 0.1 copy.47
  17.6 0.2 fusion.26
  17.8 71.3 %all_gather.14 = bf16[2,32,16,128]{3,2,1,0:T(8,128)(2,1)S(1)} all-gather(bf16[2,1,16,128]{3,2,1,0:T(8,128)(2,1)S(1)} %pad_maximum_fusion.2), channel_id=1, replica_groups=mesh['seg'=16,'blk'=2] {'seg','blk'}, dimensions={1}, use_global_device_ids=true | all-gather | bytes 270336 | tf_op jit(solution)/shard_map/all_gather | solution.py:135
  89.2 0.2 fusion.32
  89.4 0.1 multiply_reduce_fusion.1
  89.5 0.2 fusion.53
  89.7 0.2 fusion.30
  89.8 0.1 broadcast_divide_fusion
  89.9 0.0 collective-permute-done
  90.0 0.1 collective-permute-start.1
  90.1 0.1 broadcast_in_dim.103
  90.2 6.2 %collective-permute-done.1 = bf16[2,32,16,128]{3,1,2,0:T(8,128)(2,1)S(1)} collective-permute-done((bf16[2,32,16,128]{3,1,2,0:T(8,128)(2,1)S(1)}, bf16[2,32,16,128]{3,1,2,0:T(8,128)(2,1)S(1)}, u32[]{:S(2)}, u32[]{:S(2)}) %collective-permute-start.1) | collective-permute-done | bytes 262176 | tf_op jit(solution)/shard_map/ppermute | solution.py:18
  96.4 0.3 fusion.57
  96.7 0.2 fusion.35
  96.9 0.2 fusion.6
  97.2 0.1 broadcast_in_dim.109
  97.3 1.4 %copy.22 = f32[128,16,128]{0,2,1:T(8,128)} copy(f32[128,16,128]{2,1,0:T(8,128)S(1)} %bitcast.147) | data formatting | bytes 2097152 | tf_op jit(solution)/shard_map/jit(_where)/broadcast_in_dim | solution.py:74
  98.7 0.1 broadcast_in_dim.104
  98.8 0.1 broadcast_in_dim.105
  98.9 0.0 all-gather.3.cloned.1.call-done
  98.9 1.7 %multiply_reduce_fusion = (f32[16,128]{1,0:T(8,128)S(1)}, f32[16,128,256]{2,1,0:T(8,128)S(1)}) fusion(bf16[256,16,128]{0,2,1:T(8,128)(2,1)} %bitcast.154, bf16[128,2048]{1,0:T(8,128)(2,1)S(1)} %copy-done), kind=kOutput, calls=%fused_computation.1 | convolution fusion | flops 135264256 | bytes 3678208 | tf_op jit(solution)/shard_map/qhd,khd->hqk/dot_general | solution.py:48
  100.7 0.7 fusion.1
  101.4 0.1 add_add_fusion
  101.5 0.0 all-gather.5.cloned.1.call-done
  101.5 2.3 %copy.20 = bf16[256,2048]{0,1:T(8,128)(2,1)} copy(bf16[256,2048]{1,0:T(8,128)(2,1)} %all-gather.5.cloned.1.call-done) | data formatting | bytes 2097152 | tf_op jit(solution)/shard_map/all_gather | solution.py:101
  103.8 2.4 %divide_convert_fusion = bf16[128,16,128]{0,2,1:T(8,128)(2,1)S(1)} fusion(f32[128,16,128]{0,2,1:T(8,128)} %copy.22, bf16[256,16,128]{0,2,1:T(8,128)(2,1)} %bitcast.155, f32[16,128,256]{2,1,0:T(8,128)S(1)} %get-tuple-element.20, f32[16,128]{1,0:T(8,128)S(1)} %broadcast_maximum_fusion, f32[128,16]{0,1:T(8,128)S(1)} %get-tuple-element.5, ...), kind=kOutput, calls=%fused_computation.12 | convolution fusion | flops 138412032 | bytes 4780032 | tf_op jit(solution)/shard_map/hqk,khd->hqd/dot_general | solution.py:54
  106.2 1.0 copy.23
  (16 shorter events, 0.2 us)
Async XLA Ops:
  6.5 3.4 %copy-start.1 = (bf16[128,2048]{1,0:T(8,128)(2,1)S(1)}, bf16[128,2048]{1,0:T(8,128)(2,1)}, u32[]{:S(2)}) copy-start(bf16[128,2048]{1,0:T(8,128)(2,1)} %param.6) | copy-start | bytes 1572868
  6.5 3.6 %copy-start.4 = (s32[16]{0:T(128)S(1)}, s32[16]{0:T(128)}, u32[]{:S(2)}) copy-start(s32[16]{0:T(128)} %param.8) | copy-start | bytes 196
  6.5 92.4 %all-gather.3.cloned.1.call-start = ((), (), s32[]{:S(2)}) async-start(), calls=%async_computation | async-start | bytes 1572864 | tf_op jit(solution)/shard_map/all_gather | solution.py:100
  8.7 92.8 %all-gather.5.cloned.1.call-start = ((), (), s32[]{:S(2)}) async-start(), calls=%async_computation.1 | async-start | bytes 1572864 | tf_op jit(solution)/shard_map/all_gather | solution.py:101
  8.7 7.9 %copy-start.3 = (s32[16]{0:T(128)S(1)}, s32[16]{0:T(128)}, u32[]{:S(2)}) copy-start(s32[16]{0:T(128)} %param.9) | copy-start | bytes 196
  8.7 8.0 %copy-start.2 = (bf16[128,2048]{1,0:T(8,128)(2,1)S(1)}, bf16[128,2048]{1,0:T(8,128)(2,1)}, u32[]{:S(2)}) copy-start(bf16[128,2048]{1,0:T(8,128)(2,1)} %param.7) | copy-start | bytes 1572868
  10.0 7.2 %copy-start = (bf16[128,2048]{1,0:T(8,128)(2,1)S(1)}, bf16[128,2048]{1,0:T(8,128)(2,1)}, u32[]{:S(2)}) copy-start(bf16[128,2048]{1,0:T(8,128)(2,1)} %param.5) | copy-start | bytes 1572868
  16.6 73.3 %collective-permute-start = (bf16[2,16,16,128]{3,1,2,0:T(8,128)(2,1)S(1)}, bf16[2,16,16,128]{3,1,2,0:T(8,128)(2,1)S(1)}, u32[]{:S(2)}, u32[]{:S(2)}) collective-permute-start(bf16[2,16,16,128]{3,1,2,0:T(8,128)(2,1)S(1)} %all_gather.13), channel_id=1, source_target_pairs={{0,2},{2,0},{4,6},{6,4},{8,10},{10,8},{12,14},{14,12},{16,18},{18,... | collective-permute-start | bytes 393224 | tf_op jit(solution)/shard_map/ppermute | solution.py:18
  90.0 6.4 %collective-permute-start.1 = (bf16[2,32,16,128]{3,1,2,0:T(8,128)(2,1)S(1)}, bf16[2,32,16,128]{3,1,2,0:T(8,128)(2,1)S(1)}, u32[]{:S(2)}, u32[]{:S(2)}) collective-permute-start(bf16[2,32,16,128]{3,1,2,0:T(8,128)(2,1)S(1)} %pad_maximum_fusion), channel_id=1, source_target_pairs={{0,4},{2,6},{4,0},{6,2},{8,12},{10,14},{12,8},{14,10},{16,20},{18,... | collective-permute-start | bytes 786440 | tf_op jit(solution)/shard_map/ppermute | solution.py:18
Sparse Core Ops, SparseCore 0:
  8.9 24.9 all-gather.2
  35.4 22.6 all-gather.4
where the time goes:
time: 114 us
  blocking collectives  77.2 us (68%)
  between operations  13.7 us (12%)
  local copies, waits for them, and re-layouts  8.74 us (8%)
  matrix products  6.45 us (6%)
  waiting for transfers between devices  6.26 us (5%)
  other arithmetic  1.62 us (1%)
    all_gather x1, blocking collectives, on_device(): piece_rows = lax.all_gather(far_pairs, ('seg', 'blk'), axis=1, tiled=True)  71.3 us
    ppermute x2, waiting for transfers between devices, from_partner(): lax.ppermute(shard, axis, [(i, i ^ 1 << bit) for i in range(lax.axis_size...  6.19 us
    all_gather x1, blocking collectives, on_device(): mid_pairs = lax.all_gather(mid_pairs, 'blk', axis=1, tiled=True)  5.89 us
    unnamed x16, local copies, waits for them, and re-layouts  3.61 us
    dot_general x2, matrix products, online_step(): jnp.einsum('hqk,khd->hqd', weights.astype(jnp.bfloat16), value_rows, pref...  2.59 us
  transfers between devices with their start and end apart: 4, of which 1 were waited for; matrix products, arithmetic and copies ran while one was open for 8% of the time, Pallas kernels for 0%

commit v1 on v0

v1 whole, which is shorter than its diff:
```python
import functools
import math

import jax
import jax.numpy as jnp
from jax import lax
from jax.experimental import pallas as pl
from jax.experimental.pallas import tpu as pltpu
from jax.sharding import PartitionSpec as P

HEADS = 16
DH = 128
SPAN = 4
MID_RATE = 16
HALF = HEADS // 2
MIDW = HALF * DH
CHUNK = 2
EARLY = 1

very_low = -1e30
MESH = pl.DeviceIdType.MESH
SCALE = math.log2(math.e) / math.sqrt(DH)


def dot_nt(a, b):
    return lax.dot_general(a, b, (((1,), (1,)), ((), ())), preferred_element_type=jnp.float32)


def dot_nn(a, b):
    return jnp.dot(a, b, preferred_element_type=jnp.float32)


def kernel(
    segs, blks, q_hbm, k_hbm, v_hbm, mid_ref, far_ref, out_hbm,
    qbuf, kbuf, vbuf, obuf, pack, far, fnum, ftop, fden,
    load_sem, store_sem, kv_send, kv_recv, y_send, y_recv, s_send, s_recv, z_send, z_recv,
):
    rows = qbuf.shape[0]
    per_dev = rows // MID_RATE
    groups = segs // SPAN
    n_chunks = HEADS // CHUNK
    cw = CHUNK * DH
    seg = lax.axis_index("seg")
    blk = lax.axis_index("blk")
    group = seg // SPAN
    place = seg % SPAN

    blk_peers = [(seg, (blk + k) % blks) for k in range(1, blks)]
    span_peers = [(group * SPAN + (place + k) % SPAN, blk) for k in range(1, SPAN)]
    far_peers = [(((group + k) % groups) * SPAN + place, blk) for k in range(1, groups)]

    barrier = pltpu.get_barrier_semaphore()
    peers = blk_peers + span_peers + far_peers
    for peer in peers:
        pl.semaphore_signal(barrier, inc=1, device_id=peer, device_id_type=MESH)

    loads = [
        pltpu.make_async_copy(k_hbm, kbuf.at[blk], load_sem.at[0]),
        pltpu.make_async_copy(v_hbm, vbuf.at[blk], load_sem.at[1]),
        pltpu.make_async_copy(q_hbm, qbuf, load_sem.at[2]),
    ]
    for load in loads:
        load.start()
    pl.semaphore_wait(barrier, len(peers))

    def kv_copy(k, c, which):
        cols = pl.ds(pl.multiple_of(c * cw, cw), cw)
        src, dst = ((k_hbm, kbuf), (v_hbm, vbuf))[which]
        return pltpu.make_async_remote_copy(
            src_ref=src.at[:, cols],
            dst_ref=dst.at[blk, :, cols],
            send_sem=kv_send.at[k, c, which],
            recv_sem=kv_recv.at[k, c, which],
            device_id=blk_peers[k],
            device_id_type=MESH,
        )

    def start_chunk(c):
        for k in range(blks - 1):
            for which in range(2):
                kv_copy(k, c, which).start()

    for c in range(EARLY):
        start_chunk(c)

    loads[0].wait()
    loads[1].wait()

    row = lax.broadcasted_iota(jnp.int32, (2 * HEADS, rows), 0)
    col = lax.broadcasted_iota(jnp.int32, (2 * HEADS, rows), 1)
    is_mid = row < HEADS
    mid_at = (row % per_dev) * MID_RATE

    def one_hot(h):
        mid_hit = is_mid & (row // per_dev == h // HALF) & (col == mid_at + mid_ref[h])
        far_hit = (row == HEADS + h) & (col == far_ref[h])
        return jnp.where(mid_hit | far_hit, 1.0, 0.0).astype(jnp.bfloat16)

    far_kv = jnp.zeros((HEADS, 2 * DH), jnp.float32)
    hots = []
    for g in range(HALF):
        lo = slice(g * DH, (g + 1) * DH)
        hi = slice((g + HALF) * DH, (g + HALF + 1) * DH)
        hot = jnp.concatenate([one_hot(g), one_hot(g + HALF)], axis=1)
        hots.append(hot)
        field = jnp.concatenate(
            [
                jnp.concatenate([kbuf[blk, :, lo], vbuf[blk, :, lo]], axis=1),
                jnp.concatenate([kbuf[blk, :, hi], vbuf[blk, :, hi]], axis=1),
            ],
            axis=0,
        )
        picked = dot_nn(hot, field)
        mid_kv = picked[:HEADS].astype(jnp.bfloat16)
        pack[place, blk, 0, :, lo] = mid_kv[:, :DH]
        pack[place, blk, 1, :, lo] = mid_kv[:, DH:]
        far_kv = far_kv + picked[HEADS:]
    far_kv = far_kv.astype(jnp.bfloat16)
    pack[place, blk, 0, :, MIDW:] = far_kv[:, :DH]
    pack[place, blk, 1, :, MIDW:] = far_kv[:, DH:]

    y_copies = [
        pltpu.make_async_remote_copy(
            src_ref=pack.at[place, blk],
            dst_ref=pack.at[place, blk],
            send_sem=y_send.at[k],
            recv_sem=y_recv.at[k],
            device_id=blk_peers[k],
            device_id_type=MESH,
        )
        for k in range(blks - 1)
    ]
    for copy in y_copies:
        copy.start()
    for c in range(EARLY, n_chunks):
        start_chunk(c)

    loads[2].wait()
    far_q = jnp.zeros((HEADS, DH), jnp.float32)
    for g in range(HALF):
        lo = slice(g * DH, (g + 1) * DH)
        hi = slice((g + HALF) * DH, (g + HALF + 1) * DH)
        field = jnp.concatenate([qbuf[:, lo], qbuf[:, hi]], axis=0)
        far_q = far_q + dot_nn(hots[g][HEADS:], field)
    far_q = far_q.astype(jnp.bfloat16)

    for copy in y_copies:
        copy.wait_recv()
    s_copies = [
        pltpu.make_async_remote_copy(
            src_ref=pack.at[place],
            dst_ref=pack.at[place],
            send_sem=s_send.at[k],
            recv_sem=s_recv.at[k],
            device_id=span_peers[k],
            device_id_type=MESH,
        )
        for k in range(SPAN - 1)
    ]
    for copy in s_copies:
        copy.start()
    for copy in s_copies:
        copy.wait_recv()

    far[group] = pack[:, :, :, :, MIDW:]
    z_copies = [
        pltpu.make_async_remote_copy(
            src_ref=far.at[group],
            dst_ref=far.at[group],
            send_sem=z_send.at[k],
            recv_sem=z_recv.at[k],
            device_id=far_peers[k],
            device_id_type=MESH,
        )
        for k in range(groups - 1)
    ]
    for copy in z_copies:
        copy.start()
    for copy in z_copies:
        copy.wait_recv()

    n_far = segs * blks * HEADS
    far_keys = far[:, :, :, 0].reshape(n_far, DH)
    far_values = far[:, :, :, 1].reshape(n_far, DH)
    far_scores = dot_nt(far_q, far_keys)
    far_row = lax.broadcasted_iota(jnp.int32, (HEADS, n_far), 0)
    far_col = lax.broadcasted_iota(jnp.int32, (HEADS, n_far), 1)
    far_scores = jnp.where(far_col % HEADS == far_row, far_scores, very_low)
    far_top = jnp.max(far_scores, axis=1, keepdims=True)
    far_weights = jnp.exp2((far_scores - far_top) * SCALE)
    fden[...] = jnp.broadcast_to(jnp.sum(far_weights, axis=1, keepdims=True), (HEADS, DH))
    ftop[...] = jnp.broadcast_to(far_top, (HEADS, DH))
    fnum[...] = dot_nn(far_weights.astype(jnp.bfloat16), far_values)

    n_mid = SPAN * blks * 2 * per_dev
    mid_lane = lax.broadcasted_iota(jnp.int32, (rows, n_mid), 1) % (2 * per_dev) // per_dev
    mid_row = lax.broadcasted_iota(jnp.int32, (rows, n_mid), 0) % MID_RATE
    far_at = lax.broadcasted_iota(jnp.int32, (rows, DH), 0)

    def attend(h):
        cols = pl.ds(pl.multiple_of(h * DH, DH), DH)
        mid_cols = pl.ds(pl.multiple_of(h % HALF * DH, DH), DH)
        query = qbuf[:, cols]
        dense_scores = dot_nt(query, kbuf[:, :, cols].reshape(blks * rows, DH))
        mid_scores = dot_nt(query, pack[:, :, 0, :, mid_cols].reshape(n_mid, DH))
        mid_ok = (mid_lane == h // HALF) & (mid_row == mid_ref[h])
        mid_scores = jnp.where(mid_ok, mid_scores, very_low)
        scores = jnp.concatenate([dense_scores, mid_scores], axis=1)
        one_top = jnp.max(scores, axis=1, keepdims=True)
        far_hit = far_at == far_ref[h]
        far_low = jnp.where(far_hit, ftop[pl.ds(h, 1), :], very_low)
        top = jnp.maximum(one_top, far_low)
        weights = jnp.exp2((scores - top[:, :1]) * SCALE)
        far_weight = jnp.exp2((far_low - top) * SCALE)
        total = jnp.sum(weights, axis=1, keepdims=True) + far_weight * fden[pl.ds(h, 1), :]
        probs = weights.astype(jnp.bfloat16)
        mixed = dot_nn(probs[:, : blks * rows], vbuf[:, :, cols].reshape(blks * rows, DH))
        mixed = mixed + dot_nn(
            probs[:, blks * rows :], pack[:, :, 1, :, mid_cols].reshape(n_mid, DH)
        )
        mixed = mixed + far_weight * fnum[pl.ds(h, 1), :]
        obuf[:, cols] = (mixed / total).astype(jnp.bfloat16)

    def out_copy(c):
        cols = pl.ds(pl.multiple_of(c * cw, cw), cw)
        return pltpu.make_async_copy(obuf.at[:, cols], out_hbm.at[:, cols], store_sem.at[c])

    def chunk_step(c, carry):
        for k in range(blks - 1):
            for which in range(2):
                kv_copy(k, c, which).wait_recv()
        for j in range(CHUNK):
            attend(c * CHUNK + j)
        out_copy(c).start()
        return carry

    lax.fori_loop(0, n_chunks, chunk_step, 0)

    for copy in y_copies + s_copies + z_copies:
        copy.wait_send()

    def finish(c, carry):
        for k in range(blks - 1):
            for which in range(2):
                kv_copy(k, c, which).wait_send()
        out_copy(c).wait()
        return carry

    lax.fori_loop(0, n_chunks, finish, 0)


def on_device(segs, blks, queries, keys, values, mid_offset, far_offset):
    rows, width = queries.shape
    groups = segs // SPAN
    n_chunks = HEADS // CHUNK
    bf16, f32 = jnp.bfloat16, jnp.float32
    dma = pltpu.SemaphoreType.DMA
    any_spec = pl.BlockSpec(memory_space=pl.ANY)
    smem_spec = pl.BlockSpec(memory_space=pltpu.SMEM)
    return pl.pallas_call(
        functools.partial(kernel, segs, blks),
        out_shape=jax.ShapeDtypeStruct((rows, width), bf16),
        in_specs=[any_spec, any_spec, any_spec, smem_spec, smem_spec],
        out_specs=any_spec,
        scratch_shapes=[
            pltpu.VMEM((rows, width), bf16),
            pltpu.VMEM((blks, rows, width), bf16),
            pltpu.VMEM((blks, rows, width), bf16),
            pltpu.VMEM((rows, width), bf16),
            pltpu.VMEM((SPAN, blks, 2, HEADS, MIDW + DH), bf16),
            pltpu.VMEM((groups, SPAN, blks, 2, HEADS, DH), bf16),
            pltpu.VMEM((HEADS, DH), f32),
            pltpu.VMEM((HEADS, DH), f32),
            pltpu.VMEM((HEADS, DH), f32),
            dma((3,)),
            dma((n_chunks,)),
            dma((blks - 1, n_chunks, 2)),
            dma((blks - 1, n_chunks, 2)),
            dma((blks - 1,)),
            dma((blks - 1,)),
            dma((SPAN - 1,)),
            dma((SPAN - 1,)),
            dma((groups - 1,)),
            dma((groups - 1,)),
        ],
        compiler_params=pltpu.CompilerParams(
            collective_id=0, has_side_effects=True, vmem_limit_bytes=63 * 1024 * 1024
        ),
    )(queries, keys, values, mid_offset, far_offset)


def solution(mesh):
    spec = P(("seg", "blk"), None)
    return jax.shard_map(
        functools.partial(on_device, mesh.shape["seg"], mesh.shape["blk"]),
        mesh=mesh,
        in_specs=(spec, spec, spec, P(), P()),
        out_specs=spec,
        check_vma=False,
    )
```

time: 114 us -> 36 us (0.32)
  blocking collectives: 77.2 us -> 0 us
  Pallas kernels: 0 us -> 33.9 us
  between operations: 13.7 us -> 0.01 us
  local copies, waits for them, and re-layouts: 8.74 us -> 1.88 us
  matrix products: 6.45 us -> 0 us
  waiting for transfers between devices: 6.26 us -> 0 us
  other arithmetic: 1.62 us -> 0 us
    all_gather x2 -> x0, blocking collectives: 77.2 us -> none  [the longest x1 71.3 us: on_device(): piece_rows = lax.all_gather(far_pairs, ('seg', 'blk'), axis=1, tiled=True)]
    pallas_call x0 -> x1, Pallas kernels: none -> 33.9 us  [on_device(): pl.pallas_call(functools.partial(kernel, segs, blks), out_shape=jax.Shape...]
    dot_general x12 -> x0, matrix products: 6.45 us -> none  [the longest x2 2.59 us: online_step(): jnp.einsum('hqk,khd->hqd', weights.astype(jnp.bfloat16), value_rows, pref...]
    ppermute x2 -> x0, waiting for transfers between devices: 6.19 us -> none  [from_partner(): lax.ppermute(shard, axis, [(i, i ^ 1 << bit) for i in range(lax.axis_size...]
    all_gather x1 -> x0, local copies, waits for them, and re-layouts: 2.28 us -> none  [on_device(): lax.all_gather(values, 'blk', axis=0, tiled=True)]
    broadcast_in_dim x6 -> x0, local copies, waits for them, and re-layouts: 1.78 us -> none  [the longest x2 1.51 us: combine_levels(): jnp.where(mid_hit[None, :, :, None], mid_out[:, None], 0.0)]
    unnamed x16 -> x1, local copies, waits for them, and re-layouts: 3.61 us -> 1.88 us
  transfers between devices with their start and end apart: 4 -> 0, of which waited for: 1 -> 0; matrix products, arithmetic and copies ran while one was open for 8% -> 0% of each run, Pallas kernels for 0% -> 0%
where the time goes in v1:
time: 36 us; the launch traced here: 35.8 us
  Pallas kernels  33.9 us (94%)
  local copies, waits for them, and re-layouts  1.88 us (5%)
    pallas_call x1, Pallas kernels, on_device(): pl.pallas_call(functools.partial(kernel, segs, blks), out_shape=jax.Shape...  33.9 us
    unnamed x1, local copies, waits for them, and re-layouts  1.88 us

profile of v1, /device:TPU:0, one launch (start us, length us, event | category | flops | bytes accessed | tf_op | source)
XLA Modules:
  0.0 35.8 jit_solution(9649305440560802881)
XLA Ops:
  0.0 33.9 %shard_map.55 = bf16[128,2048]{1,0:T(8,128)(2,1)} custom-call(bf16[128,2048]{1,0:T(8,128)(2,1)} %q_hbm.1, bf16[128,2048]{1,0:T(8,128)(2,1)} %k_hbm.1, bf16[128,2048]{1,0:T(8,128)(2,1)} %v_hbm.1, s32[16]{0:T(128)} %mid_ref.1, s32[16]{0:T(128)} %far_ref.1), custom_call_target="tpu_custom_call" | custom-call | tf_op jit(solution)/shard_map/pallas_call | solution.py:260
  33.9 1.9 %copy.7 = bf16[128,2048]{1,0:T(8,128)(2,1)} copy(bf16[128,2048]{1,0:T(8,128)(2,1)} %shard_map.55) | data formatting | bytes 1048576

commit v2 on v1

--- a/solution.py
+++ b/solution.py
@@ -31,9 +31,9 @@
 
 
 def kernel(
-    segs, blks, q_hbm, k_hbm, v_hbm, mid_ref, far_ref, out_hbm,
-    qbuf, kbuf, vbuf, obuf, pack, far, fnum, ftop, fden,
-    load_sem, store_sem, kv_send, kv_recv, y_send, y_recv, s_send, s_recv, z_send, z_recv,
+    segs, blks, q_hbm, k_hbm, v_hbm, mid_ref, far_ref, out_ref,
+    qbuf, kbuf, vbuf, pack, far, fnum, ftop, fden,
+    load_sem, kv_send, kv_recv, y_send, y_recv, s_send, s_recv, z_send, z_recv,
 ):
     rows = qbuf.shape[0]
     per_dev = rows // MID_RATE
@@ -219,11 +219,7 @@
             probs[:, blks * rows :], pack[:, :, 1, :, mid_cols].reshape(n_mid, DH)
         )
         mixed = mixed + far_weight * fnum[pl.ds(h, 1), :]
-        obuf[:, cols] = (mixed / total).astype(jnp.bfloat16)
-
-    def out_copy(c):
-        cols = pl.ds(pl.multiple_of(c * cw, cw), cw)
-        return pltpu.make_async_copy(obuf.at[:, cols], out_hbm.at[:, cols], store_sem.at[c])
+        out_ref[:, cols] = (mixed / total).astype(jnp.bfloat16)
 
     def chunk_step(c, carry):
         for k in range(blks - 1):
@@ -231,7 +227,6 @@
                 kv_copy(k, c, which).wait_recv()
         for j in range(CHUNK):
             attend(c * CHUNK + j)
-        out_copy(c).start()
         return carry
 
     lax.fori_loop(0, n_chunks, chunk_step, 0)
@@ -243,7 +238,6 @@
         for k in range(blks - 1):
             for which in range(2):
                 kv_copy(k, c, which).wait_send()
-        out_copy(c).wait()
         return carry
 
     lax.fori_loop(0, n_chunks, finish, 0)
@@ -259,21 +253,19 @@
     smem_spec = pl.BlockSpec(memory_space=pltpu.SMEM)
     return pl.pallas_call(
         functools.partial(kernel, segs, blks),
-        out_shape=jax.ShapeDtypeStruct((rows, width), bf16),
+        out_shape=pltpu.VMEM((rows, width), bf16),
         in_specs=[any_spec, any_spec, any_spec, smem_spec, smem_spec],
-        out_specs=any_spec,
+        out_specs=pl.BlockSpec(memory_space=pltpu.VMEM),
         scratch_shapes=[
             pltpu.VMEM((rows, width), bf16),
             pltpu.VMEM((blks, rows, width), bf16),
             pltpu.VMEM((blks, rows, width), bf16),
-            pltpu.VMEM((rows, width), bf16),
             pltpu.VMEM((SPAN, blks, 2, HEADS, MIDW + DH), bf16),
             pltpu.VMEM((groups, SPAN, blks, 2, HEADS, DH), bf16),
             pltpu.VMEM((HEADS, DH), f32),
             pltpu.VMEM((HEADS, DH), f32),
             pltpu.VMEM((HEADS, DH), f32),
             dma((3,)),
-            dma((n_chunks,)),
             dma((blks - 1, n_chunks, 2)),
             dma((blks - 1, n_chunks, 2)),
             dma((blks - 1,)),
@@ -284,7 +276,7 @@
             dma((groups - 1,)),
         ],
         compiler_params=pltpu.CompilerParams(
-            collective_id=0, has_side_effects=True, vmem_limit_bytes=63 * 1024 * 1024
+            collective_id=0, has_side_effects=True, vmem_limit_bytes=62 * 1024 * 1024
         ),
     )(queries, keys, values, mid_offset, far_offset)
 

time: 36 us -> 34.3 us (0.953)
  local copies, waits for them, and re-layouts: 1.88 us -> 0.8 us
  Pallas kernels: 33.9 us -> 33.3 us
    unnamed x1, local copies, waits for them, and re-layouts: 1.88 us -> 0.8 us
    pallas_call x1, Pallas kernels: 33.9 us -> 33.3 us  [on_device(): pl.pallas_call(functools.partial(kernel, segs, blks), out_shape=pltpu.VME...]
where the time goes in v2:
time: 34.3 us; the launch traced here: 34.1 us
  Pallas kernels  33.3 us (97%)
  local copies, waits for them, and re-layouts  0.8 us (2%)
    pallas_call x1, Pallas kernels, on_device(): pl.pallas_call(functools.partial(kernel, segs, blks), out_shape=pltpu.VME...  33.3 us
    unnamed x1, local copies, waits for them, and re-layouts  0.8 us

profile of v2, /device:TPU:0, one launch (start us, length us, event | category | flops | bytes accessed | tf_op | source)
XLA Modules:
  0.0 34.1 jit_solution(10718795706217334681)
XLA Ops:
  0.0 33.3 %shard_map.55 = bf16[128,2048]{1,0:T(8,128)(2,1)S(1)} custom-call(bf16[128,2048]{1,0:T(8,128)(2,1)} %q_hbm.1, bf16[128,2048]{1,0:T(8,128)(2,1)} %k_hbm.1, bf16[128,2048]{1,0:T(8,128)(2,1)} %v_hbm.1, s32[16]{0:T(128)} %mid_ref.1, s32[16]{0:T(128)} %far_ref.1), custom_call_target="tpu_custom_call" | custom-call | tf_op jit(solution)/shard_map/pallas_call | solution.py:254
  33.3 0.8 %copy.7 = bf16[128,2048]{1,0:T(8,128)(2,1)} copy(bf16[128,2048]{1,0:T(8,128)(2,1)S(1)} %shard_map.55) | data formatting | bytes 1048576

commit v3 on v2

--- a/solution.py
+++ b/solution.py
@@ -33,7 +33,7 @@
 def kernel(
     segs, blks, q_hbm, k_hbm, v_hbm, mid_ref, far_ref, out_ref,
     qbuf, kbuf, vbuf, pack, far, fnum, ftop, fden,
-    load_sem, kv_send, kv_recv, y_send, y_recv, s_send, s_recv, z_send, z_recv,
+    hello_sem, wide_sem, load_sem, kv_send, kv_recv, y_send, y_recv, s_send, s_recv, z_send, z_recv,
 ):
     rows = qbuf.shape[0]
     per_dev = rows // MID_RATE
@@ -50,9 +50,20 @@
     far_peers = [(((group + k) % groups) * SPAN + place, blk) for k in range(1, groups)]
 
     barrier = pltpu.get_barrier_semaphore()
-    peers = blk_peers + span_peers + far_peers
-    for peer in peers:
-        pl.semaphore_signal(barrier, inc=1, device_id=peer, device_id_type=MESH)
+    wide = span_peers + far_peers
+    paired = blks == 2
+
+    def greet(sem, devices):
+        for device in devices:
+            pl.semaphore_signal(sem, inc=1, device_id=device, device_id_type=MESH)
+
+    if paired:
+
+        @pl.when(blk == 1)
+        def _():
+            greet(barrier, blk_peers)
+    else:
+        greet(barrier, blk_peers + wide)
 
     loads = [
         pltpu.make_async_copy(k_hbm, kbuf.at[blk], load_sem.at[0]),
@@ -61,7 +72,19 @@
     ]
     for load in loads:
         load.start()
-    pl.semaphore_wait(barrier, len(peers))
+    if paired:
+
+        @pl.when(blk == 0)
+        def _():
+            pl.semaphore_wait(barrier, 1)
+            greet(hello_sem, blk_peers)
+
+        @pl.when(blk == 1)
+        def _():
+            pl.semaphore_wait(hello_sem, 1)
+            greet(barrier, wide)
+    else:
+        pl.semaphore_wait(barrier, len(blk_peers) + len(wide))
 
     def kv_copy(k, c, which):
         cols = pl.ds(pl.multiple_of(c * cw, cw), cw)
@@ -134,6 +157,17 @@
         copy.start()
     for c in range(EARLY, n_chunks):
         start_chunk(c)
+
+    if paired:
+
+        @pl.when(blk == 1)
+        def _():
+            pl.semaphore_wait(barrier, len(wide))
+            greet(wide_sem, blk_peers)
+
+        @pl.when(blk == 0)
+        def _():
+            pl.semaphore_wait(wide_sem, 1)
 
     loads[2].wait()
     far_q = jnp.zeros((HEADS, DH), jnp.float32)
@@ -265,6 +299,8 @@
             pltpu.VMEM((HEADS, DH), f32),
             pltpu.VMEM((HEADS, DH), f32),
             pltpu.VMEM((HEADS, DH), f32),
+            pltpu.SemaphoreType.REGULAR,
+            pltpu.SemaphoreType.REGULAR,
             dma((3,)),
             dma((blks - 1, n_chunks, 2)),
             dma((blks - 1, n_chunks, 2)),

time: 34.3 us -> 33.4 us (0.974)
  the two profiles are of different devices: /device:TPU:0 before, /device:TPU:1 now
where the time goes in v3:
time: 33.4 us; the launch traced here: 33.2 us
  Pallas kernels  32.4 us (97%)
  local copies, waits for them, and re-layouts  0.8 us (2%)
    pallas_call x1, Pallas kernels, on_device(): pl.pallas_call(functools.partial(kernel, segs, blks), out_shape=pltpu.VME...  32.4 us
    unnamed x1, local copies, waits for them, and re-layouts  0.8 us

profile of v3, /device:TPU:1, one launch (start us, length us, event | category | flops | bytes accessed | tf_op | source)
XLA Modules:
  0.0 33.2 jit_solution(812242716862944829)
XLA Ops:
  0.0 32.4 %shard_map.55 = bf16[128,2048]{1,0:T(8,128)(2,1)S(1)} custom-call(bf16[128,2048]{1,0:T(8,128)(2,1)} %q_hbm.1, bf16[128,2048]{1,0:T(8,128)(2,1)} %k_hbm.1, bf16[128,2048]{1,0:T(8,128)(2,1)} %v_hbm.1, s32[16]{0:T(128)} %mid_ref.1, s32[16]{0:T(128)} %far_ref.1), custom_call_target="tpu_custom_call" | custom-call | tf_op jit(solution)/shard_map/pallas_call | solution.py:288
  32.4 0.8 %copy.7 = bf16[128,2048]{1,0:T(8,128)(2,1)} copy(bf16[128,2048]{1,0:T(8,128)(2,1)S(1)} %shard_map.55) | data formatting | bytes 1048576

commit v4 on v3

--- a/solution.py
+++ b/solution.py
@@ -16,6 +16,7 @@
 MIDW = HALF * DH
 CHUNK = 2
 EARLY = 1
+LATE = 1
 
 very_low = -1e30
 MESH = pl.DeviceIdType.MESH
@@ -32,8 +33,8 @@
 
 def kernel(
     segs, blks, q_hbm, k_hbm, v_hbm, mid_ref, far_ref, out_ref,
-    qbuf, kbuf, vbuf, pack, far, fnum, ftop, fden,
-    hello_sem, wide_sem, load_sem, kv_send, kv_recv, y_send, y_recv, s_send, s_recv, z_send, z_recv,
+    qbuf, kbuf, vbuf, mid, far, fnum, ftop, fden, rnum, rtop, rden,
+    hello_sem, wide_sem, load_sem, kv_send, kv_recv, y_send, y_recv, s_send, s_recv, z_send, z_recv, f_send, f_recv,
 ):
     rows = qbuf.shape[0]
     per_dev = rows // MID_RATE
@@ -135,24 +136,27 @@
         )
         picked = dot_nn(hot, field)
         mid_kv = picked[:HEADS].astype(jnp.bfloat16)
-        pack[place, blk, 0, :, lo] = mid_kv[:, :DH]
-        pack[place, blk, 1, :, lo] = mid_kv[:, DH:]
+        mid[place, blk, 0, :, lo] = mid_kv[:, :DH]
+        mid[place, blk, 1, :, lo] = mid_kv[:, DH:]
         far_kv = far_kv + picked[HEADS:]
     far_kv = far_kv.astype(jnp.bfloat16)
-    pack[place, blk, 0, :, MIDW:] = far_kv[:, :DH]
-    pack[place, blk, 1, :, MIDW:] = far_kv[:, DH:]
-
-    y_copies = [
-        pltpu.make_async_remote_copy(
-            src_ref=pack.at[place, blk],
-            dst_ref=pack.at[place, blk],
-            send_sem=y_send.at[k],
-            recv_sem=y_recv.at[k],
-            device_id=blk_peers[k],
+    far[place, group, blk, 0] = far_kv[:, :DH]
+    far[place, group, blk, 1] = far_kv[:, DH:]
+
+    def remote(ref, send_sem, recv_sem, device):
+        return pltpu.make_async_remote_copy(
+            src_ref=ref,
+            dst_ref=ref,
+            send_sem=send_sem,
+            recv_sem=recv_sem,
+            device_id=device,
             device_id_type=MESH,
         )
-        for k in range(blks - 1)
-    ]
+
+    y_copies = []
+    for k in range(blks - 1):
+        for i, ref in enumerate((far.at[place, group, blk], mid.at[place, blk])):
+            y_copies.append(remote(ref, y_send.at[k, i], y_recv.at[k, i], blk_peers[k]))
     for copy in y_copies:
         copy.start()
     for c in range(EARLY, n_chunks):
@@ -180,92 +184,116 @@
 
     for copy in y_copies:
         copy.wait_recv()
+    z_copies = [
+        remote(far.at[place, group], z_send.at[k], z_recv.at[k], far_peers[k])
+        for k in range(groups - 1)
+    ]
     s_copies = [
-        pltpu.make_async_remote_copy(
-            src_ref=pack.at[place],
-            dst_ref=pack.at[place],
-            send_sem=s_send.at[k],
-            recv_sem=s_recv.at[k],
-            device_id=span_peers[k],
-            device_id_type=MESH,
-        )
-        for k in range(SPAN - 1)
+        remote(mid.at[place], s_send.at[k], s_recv.at[k], span_peers[k]) for k in range(SPAN - 1)
     ]
-    for copy in s_copies:
+    f_copies = [
+        remote(far.at[place], f_send.at[k], f_recv.at[k], span_peers[k]) for k in range(SPAN - 1)
+    ]
+    for copy in z_copies + s_copies:
+        copy.start()
+    for copy in z_copies:
+        copy.wait_recv()
+    for copy in f_copies:
         copy.start()
     for copy in s_copies:
         copy.wait_recv()
-
-    far[group] = pack[:, :, :, :, MIDW:]
-    z_copies = [
-        pltpu.make_async_remote_copy(
-            src_ref=far.at[group],
-            dst_ref=far.at[group],
-            send_sem=z_send.at[k],
-            recv_sem=z_recv.at[k],
-            device_id=far_peers[k],
-            device_id_type=MESH,
-        )
-        for k in range(groups - 1)
-    ]
-    for copy in z_copies:
-        copy.start()
-    for copy in z_copies:
-        copy.wait_recv()
-
-    n_far = segs * blks * HEADS
-    far_keys = far[:, :, :, 0].reshape(n_far, DH)
-    far_values = far[:, :, :, 1].reshape(n_far, DH)
-    far_scores = dot_nt(far_q, far_keys)
-    far_row = lax.broadcasted_iota(jnp.int32, (HEADS, n_far), 0)
-    far_col = lax.broadcasted_iota(jnp.int32, (HEADS, n_far), 1)
-    far_scores = jnp.where(far_col % HEADS == far_row, far_scores, very_low)
-    far_top = jnp.max(far_scores, axis=1, keepdims=True)
-    far_weights = jnp.exp2((far_scores - far_top) * SCALE)
-    fden[...] = jnp.broadcast_to(jnp.sum(far_weights, axis=1, keepdims=True), (HEADS, DH))
-    ftop[...] = jnp.broadcast_to(far_top, (HEADS, DH))
-    fnum[...] = dot_nn(far_weights.astype(jnp.bfloat16), far_values)
 
     n_mid = SPAN * blks * 2 * per_dev
     mid_lane = lax.broadcasted_iota(jnp.int32, (rows, n_mid), 1) % (2 * per_dev) // per_dev
     mid_row = lax.broadcasted_iota(jnp.int32, (rows, n_mid), 0) % MID_RATE
     far_at = lax.broadcasted_iota(jnp.int32, (rows, DH), 0)
 
-    def attend(h):
+    def attend_far():
+        n_far = segs * blks * HEADS
+        far_keys = far[:, :, :, 0].reshape(n_far, DH)
+        far_values = far[:, :, :, 1].reshape(n_far, DH)
+        far_scores = dot_nt(far_q, far_keys)
+        far_row = lax.broadcasted_iota(jnp.int32, (HEADS, n_far), 0)
+        far_col = lax.broadcasted_iota(jnp.int32, (HEADS, n_far), 1)
+        far_scores = jnp.where(far_col % HEADS == far_row, far_scores, very_low)
+        far_top = jnp.max(far_scores, axis=1, keepdims=True)
+        far_weights = jnp.exp2((far_scores - far_top) * SCALE)
+        fden[...] = jnp.broadcast_to(jnp.sum(far_weights, axis=1, keepdims=True), (HEADS, DH))
+        ftop[...] = jnp.broadcast_to(far_top, (HEADS, DH))
+        fnum[...] = dot_nn(far_weights.astype(jnp.bfloat16), far_values)
+
+    def attend(h, with_far):
         cols = pl.ds(pl.multiple_of(h * DH, DH), DH)
         mid_cols = pl.ds(pl.multiple_of(h % HALF * DH, DH), DH)
         query = qbuf[:, cols]
         dense_scores = dot_nt(query, kbuf[:, :, cols].reshape(blks * rows, DH))
-        mid_scores = dot_nt(query, pack[:, :, 0, :, mid_cols].reshape(n_mid, DH))
+        mid_scores = dot_nt(query, mid[:, :, 0, :, mid_cols].reshape(n_mid, DH))
         mid_ok = (mid_lane == h // HALF) & (mid_row == mid_ref[h])
         mid_scores = jnp.where(mid_ok, mid_scores, very_low)
         scores = jnp.concatenate([dense_scores, mid_scores], axis=1)
-        one_top = jnp.max(scores, axis=1, keepdims=True)
+        top = jnp.max(scores, axis=1, keepdims=True)
         far_hit = far_at == far_ref[h]
-        far_low = jnp.where(far_hit, ftop[pl.ds(h, 1), :], very_low)
-        top = jnp.maximum(one_top, far_low)
-        weights = jnp.exp2((scores - top[:, :1]) * SCALE)
-        far_weight = jnp.exp2((far_low - top) * SCALE)
-        total = jnp.sum(weights, axis=1, keepdims=True) + far_weight * fden[pl.ds(h, 1), :]
+        if with_far:
+            far_low = jnp.where(far_hit, ftop[pl.ds(h, 1), :], very_low)
+            wide_top = jnp.maximum(top, far_low)
+            top = wide_top[:, :1]
+        weights = jnp.exp2((scores - top) * SCALE)
+        total = jnp.sum(weights, axis=1, keepdims=True)
         probs = weights.astype(jnp.bfloat16)
         mixed = dot_nn(probs[:, : blks * rows], vbuf[:, :, cols].reshape(blks * rows, DH))
         mixed = mixed + dot_nn(
-            probs[:, blks * rows :], pack[:, :, 1, :, mid_cols].reshape(n_mid, DH)
+            probs[:, blks * rows :], mid[:, :, 1, :, mid_cols].reshape(n_mid, DH)
         )
-        mixed = mixed + far_weight * fnum[pl.ds(h, 1), :]
+        if with_far:
+            far_weight = jnp.exp2((far_low - wide_top) * SCALE)
+            total = total + far_weight * fden[pl.ds(h, 1), :]
+            mixed = mixed + far_weight * fnum[pl.ds(h, 1), :]
+        else:
+            for ref, value in ((rnum, mixed), (rtop, top), (rden, total)):
+                kept = jnp.where(far_hit, value, 0.0)
+                ref[pl.ds(h, 1), :] = jnp.sum(kept, axis=0, keepdims=True)
         out_ref[:, cols] = (mixed / total).astype(jnp.bfloat16)
 
-    def chunk_step(c, carry):
+    def merge_far():
+        top = jnp.maximum(rtop[...], ftop[...])
+        near_weight = jnp.exp2((rtop[...] - top) * SCALE)
+        far_weight = jnp.exp2((ftop[...] - top) * SCALE)
+        total = near_weight * rden[...] + far_weight * fden[...]
+        rnum[...] = (near_weight * rnum[...] + far_weight * fnum[...]) / total
+
+        def put(h, carry):
+            cols = pl.ds(pl.multiple_of(h * DH, DH), DH)
+            plain = out_ref[:, cols].astype(jnp.float32)
+            merged = jnp.where(far_at == far_ref[h], rnum[pl.ds(h, 1), :], plain)
+            out_ref[:, cols] = merged.astype(jnp.bfloat16)
+            return carry
+
+        lax.fori_loop(0, HEADS - LATE * CHUNK, put, 0, unroll=2)
+
+    def await_chunk(c):
         for k in range(blks - 1):
             for which in range(2):
                 kv_copy(k, c, which).wait_recv()
+
+    def chunk_step(c, carry):
+        await_chunk(c)
         for j in range(CHUNK):
-            attend(c * CHUNK + j)
+            attend(c * CHUNK + j, False)
         return carry
 
-    lax.fori_loop(0, n_chunks, chunk_step, 0)
-
-    for copy in y_copies + s_copies + z_copies:
+    for ref in (rnum, rtop, rden):
+        ref[...] = jnp.ones_like(ref)
+    lax.fori_loop(0, n_chunks - LATE, chunk_step, 0)
+    for copy in f_copies:
+        copy.wait_recv()
+    attend_far()
+    merge_far()
+    for c in range(n_chunks - LATE, n_chunks):
+        await_chunk(c)
+        for j in range(CHUNK):
+            attend(c * CHUNK + j, True)
+
+    for copy in y_copies + s_copies + z_copies + f_copies:
         copy.wait_send()
 
     def finish(c, carry):
@@ -294,8 +322,11 @@
             pltpu.VMEM((rows, width), bf16),
             pltpu.VMEM((blks, rows, width), bf16),
             pltpu.VMEM((blks, rows, width), bf16),
-            pltpu.VMEM((SPAN, blks, 2, HEADS, MIDW + DH), bf16),
-            pltpu.VMEM((groups, SPAN, blks, 2, HEADS, DH), bf16),
+            pltpu.VMEM((SPAN, blks, 2, HEADS, MIDW), bf16),
+            pltpu.VMEM((SPAN, groups, blks, 2, HEADS, DH), bf16),
+            pltpu.VMEM((HEADS, DH), f32),
+            pltpu.VMEM((HEADS, DH), f32),
+            pltpu.VMEM((HEADS, DH), f32),
             pltpu.VMEM((HEADS, DH), f32),
             pltpu.VMEM((HEADS, DH), f32),
             pltpu.VMEM((HEADS, DH), f32),
@@ -304,12 +335,14 @@
             dma((3,)),
             dma((blks - 1, n_chunks, 2)),
             dma((blks - 1, n_chunks, 2)),
-            dma((blks - 1,)),
-            dma((blks - 1,)),
+            dma((blks - 1, 2)),
+            dma((blks - 1, 2)),
             dma((SPAN - 1,)),
             dma((SPAN - 1,)),
             dma((groups - 1,)),
             dma((groups - 1,)),
+            dma((SPAN - 1,)),
+            dma((SPAN - 1,)),
         ],
         compiler_params=pltpu.CompilerParams(
             collective_id=0, has_side_effects=True, vmem_limit_bytes=62 * 1024 * 1024

time: 33.4 us -> 32.5 us (0.973)
  the two profiles are of different devices: /device:TPU:1 before, /device:TPU:0 now
where the time goes in v4:
time: 32.5 us; the launch traced here: 32.3 us
  Pallas kernels  31.5 us (97%)
  local copies, waits for them, and re-layouts  0.8 us (2%)
    pallas_call x1, Pallas kernels, on_device(): pl.pallas_call(functools.partial(kernel, segs, blks), out_shape=pltpu.VME...  31.5 us
    unnamed x1, local copies, waits for them, and re-layouts  0.8 us

profile of v4, /device:TPU:0, one launch (start us, length us, event | category | flops | bytes accessed | tf_op | source)
XLA Modules:
  0.0 32.3 jit_solution(15792059691829975395)
XLA Ops:
  0.0 31.5 %shard_map.55 = bf16[128,2048]{1,0:T(8,128)(2,1)S(1)} custom-call(bf16[128,2048]{1,0:T(8,128)(2,1)} %q_hbm.1, bf16[128,2048]{1,0:T(8,128)(2,1)} %k_hbm.1, bf16[128,2048]{1,0:T(8,128)(2,1)} %v_hbm.1, s32[16]{0:T(128)} %mid_ref.1, s32[16]{0:T(128)} %far_ref.1), custom_call_target="tpu_custom_call" | custom-call | tf_op jit(solution)/shard_map/pallas_call | solution.py:316
  31.5 0.8 %copy.7 = bf16[128,2048]{1,0:T(8,128)(2,1)} copy(bf16[128,2048]{1,0:T(8,128)(2,1)S(1)} %shard_map.55) | data formatting | bytes 1048576

commit v5 on v4

--- a/solution.py
+++ b/solution.py
@@ -32,7 +32,8 @@
 
 
 def kernel(
-    segs, blks, q_hbm, k_hbm, v_hbm, mid_ref, far_ref, out_ref,
+    segs, blks, q_hbm, k_hbm, v_hbm, mid_hbm, far_hbm, out_ref,
+    mid_ref, far_ref,
     qbuf, kbuf, vbuf, mid, far, fnum, ftop, fden, rnum, rtop, rden,
     hello_sem, wide_sem, load_sem, kv_send, kv_recv, y_send, y_recv, s_send, s_recv, z_send, z_recv, f_send, f_recv,
 ):
@@ -70,6 +71,8 @@
         pltpu.make_async_copy(k_hbm, kbuf.at[blk], load_sem.at[0]),
         pltpu.make_async_copy(v_hbm, vbuf.at[blk], load_sem.at[1]),
         pltpu.make_async_copy(q_hbm, qbuf, load_sem.at[2]),
+        pltpu.make_async_copy(mid_hbm, mid_ref, load_sem.at[3]),
+        pltpu.make_async_copy(far_hbm, far_ref, load_sem.at[4]),
     ]
     for load in loads:
         load.start()
@@ -83,7 +86,6 @@
         @pl.when(blk == 1)
         def _():
             pl.semaphore_wait(hello_sem, 1)
-            greet(barrier, wide)
     else:
         pl.semaphore_wait(barrier, len(blk_peers) + len(wide))
 
@@ -106,9 +108,16 @@
 
     for c in range(EARLY):
         start_chunk(c)
+    if paired:
+
+        @pl.when(blk == 1)
+        def _():
+            greet(barrier, wide)
 
     loads[0].wait()
     loads[1].wait()
+    loads[3].wait()
+    loads[4].wait()
 
     row = lax.broadcasted_iota(jnp.int32, (2 * HEADS, rows), 0)
     col = lax.broadcasted_iota(jnp.int32, (2 * HEADS, rows), 1)
@@ -312,13 +321,14 @@
     bf16, f32 = jnp.bfloat16, jnp.float32
     dma = pltpu.SemaphoreType.DMA
     any_spec = pl.BlockSpec(memory_space=pl.ANY)
-    smem_spec = pl.BlockSpec(memory_space=pltpu.SMEM)
     return pl.pallas_call(
         functools.partial(kernel, segs, blks),
         out_shape=pltpu.VMEM((rows, width), bf16),
-        in_specs=[any_spec, any_spec, any_spec, smem_spec, smem_spec],
+        in_specs=[any_spec] * 5,
         out_specs=pl.BlockSpec(memory_space=pltpu.VMEM),
         scratch_shapes=[
+            pltpu.SMEM((HEADS,), jnp.int32),
+            pltpu.SMEM((HEADS,), jnp.int32),
             pltpu.VMEM((rows, width), bf16),
             pltpu.VMEM((blks, rows, width), bf16),
             pltpu.VMEM((blks, rows, width), bf16),
@@ -332,7 +342,7 @@
             pltpu.VMEM((HEADS, DH), f32),
             pltpu.SemaphoreType.REGULAR,
             pltpu.SemaphoreType.REGULAR,
-            dma((3,)),
+            dma((5,)),
             dma((blks - 1, n_chunks, 2)),
             dma((blks - 1, n_chunks, 2)),
             dma((blks - 1, 2)),

time: 32.5 us -> 31.7 us (0.975)
  Pallas kernels: 31.5 us -> 30.8 us
    pallas_call x1, Pallas kernels: 31.5 us -> 30.8 us  [on_device(): pl.pallas_call(functools.partial(kernel, segs, blks), out_shape=pltpu.VME...]
where the time goes in v5:
time: 31.7 us; the launch traced here: 31.6 us
  Pallas kernels  30.8 us (97%)
  local copies, waits for them, and re-layouts  0.8 us (3%)
    pallas_call x1, Pallas kernels, on_device(): pl.pallas_call(functools.partial(kernel, segs, blks), out_shape=pltpu.VME...  30.8 us
    unnamed x1, local copies, waits for them, and re-layouts  0.8 us

profile of v5, /device:TPU:0, one launch (start us, length us, event | category | flops | bytes accessed | tf_op | source)
XLA Modules:
  0.0 31.6 jit_solution(17065552210417307967)
XLA Ops:
  0.0 30.8 %shard_map.55 = bf16[128,2048]{1,0:T(8,128)(2,1)S(1)} custom-call(bf16[128,2048]{1,0:T(8,128)(2,1)} %q_hbm.1, bf16[128,2048]{1,0:T(8,128)(2,1)} %k_hbm.1, bf16[128,2048]{1,0:T(8,128)(2,1)} %v_hbm.1, s32[16]{0:T(128)} %mid_hbm.1, s32[16]{0:T(128)} %far_hbm.1), custom_call_target="tpu_custom_call" | custom-call | tf_op jit(solution)/shard_map/pallas_call | solution.py:324
  30.8 0.8 %copy.7 = bf16[128,2048]{1,0:T(8,128)(2,1)} copy(bf16[128,2048]{1,0:T(8,128)(2,1)S(1)} %shard_map.55) | data formatting | bytes 1048576

commit v6 on v5

--- a/solution.py
+++ b/solution.py
@@ -14,7 +14,7 @@
 MID_RATE = 16
 HALF = HEADS // 2
 MIDW = HALF * DH
-CHUNK = 2
+CHUNK = 4
 EARLY = 1
 LATE = 1
 
@@ -249,6 +249,7 @@
         weights = jnp.exp2((scores - top) * SCALE)
         total = jnp.sum(weights, axis=1, keepdims=True)
         probs = weights.astype(jnp.bfloat16)
+        yield
         mixed = dot_nn(probs[:, : blks * rows], vbuf[:, :, cols].reshape(blks * rows, DH))
         mixed = mixed + dot_nn(
             probs[:, blks * rows :], mid[:, :, 1, :, mid_cols].reshape(n_mid, DH)
@@ -279,15 +280,21 @@
 
         lax.fori_loop(0, HEADS - LATE * CHUNK, put, 0, unroll=2)
 
-    def await_chunk(c):
+    def await_chunk(c, which):
         for k in range(blks - 1):
-            for which in range(2):
-                kv_copy(k, c, which).wait_recv()
+            kv_copy(k, c, which).wait_recv()
+
+    def run_chunk(c, with_far):
+        await_chunk(c, 0)
+        heads = [attend(c * CHUNK + j, with_far) for j in range(CHUNK)]
+        for head in heads:
+            next(head)
+        await_chunk(c, 1)
+        for head in heads:
+            next(head, None)
 
     def chunk_step(c, carry):
-        await_chunk(c)
-        for j in range(CHUNK):
-            attend(c * CHUNK + j, False)
+        run_chunk(c, False)
         return carry
 
     for ref in (rnum, rtop, rden):
@@ -298,9 +305,7 @@
     attend_far()
     merge_far()
     for c in range(n_chunks - LATE, n_chunks):
-        await_chunk(c)
-        for j in range(CHUNK):
-            attend(c * CHUNK + j, True)
+        run_chunk(c, True)
 
     for copy in y_copies + s_copies + z_copies + f_copies:
         copy.wait_send()

time: 31.7 us -> 31 us (0.978)
  Pallas kernels: 30.8 us -> 30.1 us
    pallas_call x1, Pallas kernels: 30.8 us -> 30.1 us  [on_device(): pl.pallas_call(functools.partial(kernel, segs, blks), out_shape=pltpu.VME...]
where the time goes in v6:
time: 31 us; the launch traced here: 30.9 us
  Pallas kernels  30.1 us (97%)
  local copies, waits for them, and re-layouts  0.8 us (3%)
    pallas_call x1, Pallas kernels, on_device(): pl.pallas_call(functools.partial(kernel, segs, blks), out_shape=pltpu.VME...  30.1 us
    unnamed x1, local copies, waits for them, and re-layouts  0.8 us

profile of v6, /device:TPU:0, one launch (start us, length us, event | category | flops | bytes accessed | tf_op | source)
XLA Modules:
  0.0 30.9 jit_solution(1943525908738103011)
XLA Ops:
  0.0 30.1 %shard_map.55 = bf16[128,2048]{1,0:T(8,128)(2,1)S(1)} custom-call(bf16[128,2048]{1,0:T(8,128)(2,1)} %q_hbm.1, bf16[128,2048]{1,0:T(8,128)(2,1)} %k_hbm.1, bf16[128,2048]{1,0:T(8,128)(2,1)} %v_hbm.1, s32[16]{0:T(128)} %mid_hbm.1, s32[16]{0:T(128)} %far_hbm.1), custom_call_target="tpu_custom_call" | custom-call | tf_op jit(solution)/shard_map/pallas_call | solution.py:329
  30.1 0.8 %copy.7 = bf16[128,2048]{1,0:T(8,128)(2,1)} copy(bf16[128,2048]{1,0:T(8,128)(2,1)S(1)} %shard_map.55) | data formatting | bytes 1048576
